TPU v7x, 256 devices: a whole 4x4x8 slice. The times are simulated.
256 devices in a mesh: src: 16 (over y, x), tgt: 16 (over z, core).
Axes of the slice: x: 4, y: 4, z: 8, core: 2. Of those that a mesh axis runs over, the one named last changes fastest.
Arguments:
- pcs_source: bfloat16 [30, 32768], P(None, 'src'), may hold values from -6 to 10
- pcs_target: bfloat16 [30, 32768], P(None, 'tgt'), may hold values from -6 to 6
- growth: float32 [32768], P('src'), may hold values from 0.25 to 4
- scores: bfloat16 [32768, 128], P('src'), may hold values from -6 to 6
Outputs:
- source_potential: float32 [32768], P('src')
- target_potential: float32 [32768], P('tgt')
- transported: float32 [32768, 128], P('tgt')
All inputs are finite; a program needn't handle non-finite values.
Results may differ from a plain program's by a relative error of at most 0.0029.
Values sent between devices are 32-bit elements; how exact they have to be, the bound alone decides.
No kernel may reach another device: no remote copies, remote signals or barrier semaphores. Data moves between devices by JAX's collectives and lax.ppermute only.
A program may use at most 64 MiB of HBM per device.

v0:
```python
import math

import jax
import jax.numpy as jnp
from jax import lax
from jax.sharding import PartitionSpec as P

ITERS = 2


EPSILON = 0.05
MARGIN = 1.0
FACTOR = MARGIN / (MARGIN + EPSILON)


def copy_for_each(x, axis):
    length = lax.axis_size(axis)
    return lax.all_to_all(jnp.broadcast_to(x[None], (length, *x.shape)), axis, 0, 0, tiled=True)


def collected_together(x, axis):
    leaves = jax.tree.leaves(x)
    order = sorted(range(len(leaves)), key=lambda k: -leaves[k].size)
    width = (1, *leaves[order[0]].shape)[-1]
    lines = [
        jnp.pad(leaves[k].reshape(-1), (0, -leaves[k].size % width)).reshape(-1, width)
        for k in order
    ]
    both, at, found = (copy_for_each(jnp.concatenate(lines), axis), 0, {})
    for k, line in zip(order, lines):
        section = both[:, at : at + len(line)].reshape(len(both), -1)
        found[k] = section[:, : leaves[k].size].reshape(-1, *leaves[k].shape)
        at += len(line)
    numbers = iter(range(len(leaves)))
    return jax.tree.map(lambda _: found[next(numbers)], x)


def once_a_type(x, axis):
    leaves, found = (jax.tree.leaves(x), {})
    for leading, a in enumerate(leaves):
        if leading not in found:
            alike = [k for k, b in enumerate(leaves) if b.dtype == a.dtype]
            got = (
                collected_together([leaves[k] for k in alike], axis)
                if len(alike) > 1
                else [copy_for_each(a, axis)]
            )
            for k, b in zip(alike, got):
                found[k] = b
    numbers = iter(range(len(leaves)))
    return jax.tree.map(lambda _: found[next(numbers)], x)


def joined_by_halves(pieces, combine):
    while len(jax.tree.leaves(pieces)[0]) > 1:
        pieces = jax.vmap(combine)(
            *(jax.tree.map(lambda part: part[side::2], pieces) for side in (0, 1))
        )
    return jax.tree.map(lambda part: part[0], pieces)


def combined_all(x, axis, combine):
    pieces = once_a_type(x, axis)
    return joined_by_halves(pieces, combine)


def combined_all_2(x, axis, combine):
    pieces = collected_together(x, axis)
    return joined_by_halves(pieces, combine)


def cut_along(x, dim, length):
    dims = x.shape
    blocks = x.reshape(*dims[:dim], length, dims[dim] // length, *dims[dim + 1 :])
    return jnp.moveaxis(blocks, dim, 0)


def sum_at_owner(x, axis, dim):
    length = lax.axis_size(axis)
    blocks = lax.all_to_all(cut_along(x, dim, length), axis, 0, 0, tiled=True)
    return jnp.sum(blocks, axis=0)


def sent_together(arrays, axis, dim, along):
    widths = [math.prod(a.shape[along:]) for a in arrays]
    both = jnp.concatenate(
        [a.reshape(*a.shape[:along], w) for a, w in zip(arrays, widths)], axis=along
    )
    result = sum_at_owner(both, axis, dim)
    blocks = jnp.split(result, [sum(widths[:k]) for k in range(1, len(widths))], axis=along)
    return tuple(
        (b.reshape(*result.shape[:along], *a.shape[along:]) for a, b in zip(arrays, blocks))
    )


def in_order(blocks, dim):
    blocks = jnp.moveaxis(blocks, 0, dim)
    dims = blocks.shape
    return blocks.reshape(*dims[:dim], dims[dim] * dims[dim + 1], *dims[dim + 2 :])


def collect(x, axis, dim):
    blocks = copy_for_each(x, axis)
    return in_order(blocks, dim)


def cost_tile(left, right, right_sq):
    cross = lax.dot_general(
        left, right, (((0,), (0,)), ((), ())), preferred_element_type=jnp.float32
    )
    left_wide = left.astype(jnp.float32)
    left_sq = jnp.sum(left_wide * left_wide, axis=0)
    return (left_sq[:, None] + right_sq[None, :] - 2.0 * cross) / left.shape[0]


def combine(first, second):
    peak = jnp.maximum(first[0], second[0])
    total = first[1] * jnp.exp(first[0] - peak) + second[1] * jnp.exp(second[0] - peak)
    return (peak, total)


def row_reduce(peak, total):
    top, summed = combined_all((peak, total), "tgt", combine)
    return top + jnp.log(summed)


def column_reduce(peak, total):
    top, summed = combined_all_2((peak, total), "src", combine)
    return top + jnp.log(summed)


def shards(pcs_source, pcs_target, growth, scores):
    source_rows = pcs_source.shape[1]
    target_rows = pcs_target.shape[1]
    width = math.gcd(source_rows, 512)
    count_blocks = source_rows // width
    source_blocks = jnp.transpose(
        pcs_source.reshape(pcs_source.shape[0], count_blocks, width), (1, 0, 2)
    )
    score_blocks = scores.reshape(count_blocks, width, scores.shape[1])
    total_sources = source_rows * lax.axis_size("src")
    total_targets = target_rows * lax.axis_size("tgt")
    log_a = jnp.log(growth) - jnp.log(jnp.float32(total_sources))
    log_b = -jnp.log(jnp.float32(total_targets))
    target_wide = pcs_target.astype(jnp.float32)
    target_sq = jnp.sum(target_wide * target_wide, axis=0)
    source_potential = jnp.zeros((source_rows,), jnp.float32)
    target_potential = jnp.zeros((target_rows,), jnp.float32)
    for step in range(ITERS):
        gpot = target_potential

        def row_stats(block):
            logits = (gpot[None, :] - cost_tile(block, pcs_target, target_sq)) / EPSILON
            peak = jnp.max(logits, axis=1)
            return (peak, jnp.sum(jnp.exp(logits - peak[:, None]), axis=1))

        peaks, totals = lax.map(row_stats, source_blocks)
        rows = row_reduce(peaks.reshape(-1), totals.reshape(-1))
        source_potential = FACTOR * (EPSILON * log_a - EPSILON * rows)

        def column_stats(carry, inputs):
            block, fblock = inputs
            logits = (fblock[:, None] - cost_tile(block, pcs_target, target_sq)) / EPSILON
            newpeak = jnp.maximum(carry[0], jnp.max(logits, axis=0))
            total = carry[1] * jnp.exp(carry[0] - newpeak) + jnp.sum(
                jnp.exp(logits - newpeak[None, :]), axis=0
            )
            return ((newpeak, total), None)

        start = (
            jnp.full((target_rows,), -jnp.inf, jnp.float32),
            jnp.zeros((target_rows,), jnp.float32),
        )
        (cpeak, ctotal), unused = lax.scan(
            column_stats, start, (source_blocks, source_potential.reshape(count_blocks, width))
        )
        columns = column_reduce(cpeak, ctotal)
        target_potential = FACTOR * (EPSILON * log_b - EPSILON * columns)

    def carry_scores(carry, inputs):
        block, fblock, sblock = inputs
        tile = cost_tile(block, pcs_target, target_sq)
        plan = jnp.exp((fblock[:, None] + target_potential[None, :] - tile) / EPSILON)
        mass = carry[1] + jnp.sum(plan, axis=0)
        carried = carry[0] + lax.dot_general(
            plan.astype(jnp.bfloat16),
            sblock,
            (((0,), (0,)), ((), ())),
            preferred_element_type=jnp.float32,
        )
        return ((carried, mass), None)

    start = (
        jnp.zeros((target_rows, scores.shape[1]), jnp.float32),
        jnp.zeros((target_rows,), jnp.float32),
    )
    (carried, mass), unused = lax.scan(
        carry_scores,
        start,
        (source_blocks, source_potential.reshape(count_blocks, width), score_blocks),
    )
    carried, mass = sent_together((carried, mass), "src", 0, 1)
    transported = collect(carried / mass[:, None], "src", 0)
    return (source_potential, target_potential, transported)


def solution(mesh):
    in_specs = (P(None, "src"), P(None, "tgt"), P("src"), P("src", None))
    out_specs = (P("src"), P("tgt"), P("tgt", None))
    return jax.shard_map(shards, mesh=mesh, in_specs=in_specs, out_specs=out_specs, check_vma=False)
```

profile of v0, /device:TPU:8, one launch (start us, length us, event | category | flops | bytes accessed | tf_op | source)
XLA Modules:
  0.0 216.5 jit_solution(6902165883362537494)
XLA Ops:
  2.6 12.1 %while.63 = (s32[]{:T(128)}, f32[4,512]{1,0:T(4,128)S(1)}, f32[4,512]{1,0:T(4,128)S(1)}, bf16[4,30,512]{2,1,0:T(8,128)(2,1)S(1)}, f32[2048]{0:T(1024)S(1)}, /*index=5*/bf16[30,2048]{1,0:T(8,128)(2,1)}, s32[]{:T(128)}, s32[]{:T(128)}) while((s32[]{:T(128)}, f32[4,512]{1,0:T(4,128)S(1)}, f32[4,512]{1,0:T(4,128)S(1)}, ...), condition=%wide.region_5.6_spmd, body=%wide.region_1.5_spmd.sunk | while | flops 72396288 | bytes 8601701 | solution.py:157
  15.6 8.6 %all-to-all-start = ((f32[16,2,2048]{2,1,0:T(2,128)}), f32[16,2,2048]{2,1,0:T(2,128)S(1)}, u32[]{:S(2)}, u32[]{:S(2)}) async-start(f32[16,2,2048]{2,1,0:T(2,128)} %broadcast_in_dim.36), calls=%async_computation | async-start | bytes 524288 | tf_op jit(solution)/shard_map/all_to_all | solution.py:18
  24.2 11.2 %all-to-all-done = f32[16,2,2048]{2,1,0:T(2,128)S(1)} async-done(((f32[16,2,2048]{2,1,0:T(2,128)}), f32[16,2,2048]{2,1,0:T(2,128)S(1)}, u32[]{:S(2)}, u32[]{:S(2)}) %all-to-all-start) | async-done | bytes 262176 | tf_op jit(solution)/shard_map/all_to_all | solution.py:18
  36.3 27.6 %while.65 = (s32[]{:T(128)}, f32[2048]{0:T(1024)S(1)}, f32[2048]{0:T(1024)S(1)}, f32[4,512]{1,0:T(4,128)S(1)}, bf16[4,30,512]{2,1,0:T(8,128)(2,1)S(1)}, /*index=...) while((s32[]{:T(128)}, f32[2048]{0:T(1024)S(1)}, f32[2048]{0:T(1024)S(1)}, ...), condition=%wide.region_10.11_spmd.clone, body=%wide.region_6.10_spmd.clone.sunk | while | flops 72407552 | bytes 8700020 | solution.py:174
  36.3 4.0 %fusion.63 = (f32[2048]{0:T(1024)S(1)}, f32[512,2048]{1,0:T(8,128)}) fusion(bf16[30,2048]{1,0:T(8,128)(2,1)} %get-tuple-element.801, bf16[4,30,512]{2,1,0:T(8,128)(2,1)S(1)} %get-tuple-element.799, s32[]{:T(128)} %get-tuple-element.786, f32[2048]{0:T(1024)S(1)} %get-tuple-element.800, f32[512]{0:T(512)S(1)} %multiply_reduce_fusion.13, ...), kind=kOutput, calls=%fused_computation.101.clone.1 | convolution fusion | flops 70252544 | bytes 4370436 | tf_op jit(solution)/shard_map/while/body/eval_jaxpr/dot_general | solution.py:108
  43.2 4.0 %fusion.63 = (f32[2048]{0:T(1024)S(1)}, f32[512,2048]{1,0:T(8,128)}) fusion(bf16[30,2048]{1,0:T(8,128)(2,1)} %get-tuple-element.801, bf16[4,30,512]{2,1,0:T(8,128)(2,1)S(1)} %get-tuple-element.799, s32[]{:T(128)} %get-tuple-element.786, f32[2048]{0:T(1024)S(1)} %get-tuple-element.800, f32[512]{0:T(512)S(1)} %multiply_reduce_fusion.13, ...), kind=kOutput, calls=%fused_computation.101.clone.1 | convolution fusion | flops 70252544 | bytes 4370436 | tf_op jit(solution)/shard_map/while/body/eval_jaxpr/dot_general | solution.py:108
  47.3 2.8 %exponential_reduce_fusion.10 = f32[2048]{0:T(1024)S(1)} fusion(f32[512,2048]{1,0:T(8,128)} %get-tuple-element.732, f32[2048]{0:T(1024)S(1)} %select_maximum_fusion.4), kind=kLoop, calls=%fused_computation.12.clone.1 | loop fusion | flops 2095104 | bytes 4210688 | tf_op jit(solution)/shard_map/while/body/eval_jaxpr/reduce_sum | solution.py:165
  50.1 4.0 %fusion.63 = (f32[2048]{0:T(1024)S(1)}, f32[512,2048]{1,0:T(8,128)}) fusion(bf16[30,2048]{1,0:T(8,128)(2,1)} %get-tuple-element.801, bf16[4,30,512]{2,1,0:T(8,128)(2,1)S(1)} %get-tuple-element.799, s32[]{:T(128)} %get-tuple-element.786, f32[2048]{0:T(1024)S(1)} %get-tuple-element.800, f32[512]{0:T(512)S(1)} %multiply_reduce_fusion.13, ...), kind=kOutput, calls=%fused_computation.101.clone.1 | convolution fusion | flops 70252544 | bytes 4370436 | tf_op jit(solution)/shard_map/while/body/eval_jaxpr/dot_general | solution.py:108
  57.0 4.0 %fusion.63 = (f32[2048]{0:T(1024)S(1)}, f32[512,2048]{1,0:T(8,128)}) fusion(bf16[30,2048]{1,0:T(8,128)(2,1)} %get-tuple-element.801, bf16[4,30,512]{2,1,0:T(8,128)(2,1)S(1)} %get-tuple-element.799, s32[]{:T(128)} %get-tuple-element.786, f32[2048]{0:T(1024)S(1)} %get-tuple-element.800, f32[512]{0:T(512)S(1)} %multiply_reduce_fusion.13, ...), kind=kOutput, calls=%fused_computation.101.clone.1 | convolution fusion | flops 70252544 | bytes 4370436 | tf_op jit(solution)/shard_map/while/body/eval_jaxpr/dot_general | solution.py:108
  64.7 7.4 %all-to-all-start.1 = ((f32[16,2,2048]{2,1,0:T(2,128)}), f32[16,2,2048]{2,1,0:T(2,128)S(1)}, u32[]{:S(2)}, u32[]{:S(2)}) async-start(f32[16,2,2048]{2,1,0:T(2,128)} %broadcast_in_dim.37), calls=%async_computation.1 | async-start | bytes 524288 | tf_op jit(solution)/shard_map/all_to_all | solution.py:18
  72.1 7.7 %all-to-all-done.1 = f32[16,2,2048]{2,1,0:T(2,128)S(1)} async-done(((f32[16,2,2048]{2,1,0:T(2,128)}), f32[16,2,2048]{2,1,0:T(2,128)S(1)}, u32[]{:S(2)}, u32[]{:S(2)}) %all-to-all-start.1) | async-done | bytes 262176 | tf_op jit(solution)/shard_map/all_to_all | solution.py:18
  80.7 12.2 %while.64 = (s32[]{:T(128)}, f32[4,512]{1,0:T(4,128)S(1)}, f32[4,512]{1,0:T(4,128)S(1)}, f32[2048]{0:T(1024)S(1)}, bf16[4,30,512]{2,1,0:T(8,128)(2,1)S(1)}, /*in...) while((s32[]{:T(128)}, f32[4,512]{1,0:T(4,128)S(1)}, f32[4,512]{1,0:T(4,128)S(1)}, ...), condition=%wide.region_15.16_spmd, body=%wide.region_11.15_spmd.sunk | while | flops 72396288 | bytes 8609901 | solution.py:157
  93.7 3.5 %all-to-all-start.2 = ((f32[16,2,2048]{2,1,0:T(2,128)}), f32[16,2,2048]{2,1,0:T(2,128)S(1)}, u32[]{:S(2)}, u32[]{:S(2)}) async-start(f32[16,2,2048]{2,1,0:T(2,128)} %broadcast_in_dim.38), calls=%async_computation.2 | async-start | bytes 524288 | tf_op jit(solution)/shard_map/all_to_all | solution.py:18
  97.3 11.0 %all-to-all-done.2 = f32[16,2,2048]{2,1,0:T(2,128)S(1)} async-done(((f32[16,2,2048]{2,1,0:T(2,128)}), f32[16,2,2048]{2,1,0:T(2,128)S(1)}, u32[]{:S(2)}, u32[]{:S(2)}) %all-to-all-start.2) | async-done | bytes 262176 | tf_op jit(solution)/shard_map/all_to_all | solution.py:18
  109.7 27.6 %while.66 = (s32[]{:T(128)}, f32[2048]{0:T(1024)S(1)}, f32[2048]{0:T(1024)S(1)}, f32[4,512]{1,0:T(4,128)S(1)}, bf16[4,30,512]{2,1,0:T(8,128)(2,1)S(1)}, /*index=...) while((s32[]{:T(128)}, f32[2048]{0:T(1024)S(1)}, f32[2048]{0:T(1024)S(1)}, ...), condition=%wide.region_20.21_spmd.clone, body=%wide.region_16.20_spmd.clone.sunk | while | flops 72407552 | bytes 8700020 | solution.py:174
  109.8 4.0 %fusion.66 = (f32[2048]{0:T(1024)S(1)}, f32[512,2048]{1,0:T(8,128)}) fusion(bf16[30,2048]{1,0:T(8,128)(2,1)} %get-tuple-element.855, bf16[4,30,512]{2,1,0:T(8,128)(2,1)S(1)} %get-tuple-element.853, s32[]{:T(128)} %get-tuple-element.840, f32[2048]{0:T(1024)S(1)} %get-tuple-element.854, f32[512]{0:T(512)S(1)} %multiply_reduce_fusion.14, ...), kind=kOutput, calls=%fused_computation.102.clone.1 | convolution fusion | flops 70252544 | bytes 4370436 | tf_op jit(solution)/shard_map/while/body/eval_jaxpr/dot_general | solution.py:108
  116.7 4.0 %fusion.66 = (f32[2048]{0:T(1024)S(1)}, f32[512,2048]{1,0:T(8,128)}) fusion(bf16[30,2048]{1,0:T(8,128)(2,1)} %get-tuple-element.855, bf16[4,30,512]{2,1,0:T(8,128)(2,1)S(1)} %get-tuple-element.853, s32[]{:T(128)} %get-tuple-element.840, f32[2048]{0:T(1024)S(1)} %get-tuple-element.854, f32[512]{0:T(512)S(1)} %multiply_reduce_fusion.14, ...), kind=kOutput, calls=%fused_computation.102.clone.1 | convolution fusion | flops 70252544 | bytes 4370436 | tf_op jit(solution)/shard_map/while/body/eval_jaxpr/dot_general | solution.py:108
  123.6 4.0 %fusion.66 = (f32[2048]{0:T(1024)S(1)}, f32[512,2048]{1,0:T(8,128)}) fusion(bf16[30,2048]{1,0:T(8,128)(2,1)} %get-tuple-element.855, bf16[4,30,512]{2,1,0:T(8,128)(2,1)S(1)} %get-tuple-element.853, s32[]{:T(128)} %get-tuple-element.840, f32[2048]{0:T(1024)S(1)} %get-tuple-element.854, f32[512]{0:T(512)S(1)} %multiply_reduce_fusion.14, ...), kind=kOutput, calls=%fused_computation.102.clone.1 | convolution fusion | flops 70252544 | bytes 4370436 | tf_op jit(solution)/shard_map/while/body/eval_jaxpr/dot_general | solution.py:108
  130.5 4.0 %fusion.66 = (f32[2048]{0:T(1024)S(1)}, f32[512,2048]{1,0:T(8,128)}) fusion(bf16[30,2048]{1,0:T(8,128)(2,1)} %get-tuple-element.855, bf16[4,30,512]{2,1,0:T(8,128)(2,1)S(1)} %get-tuple-element.853, s32[]{:T(128)} %get-tuple-element.840, f32[2048]{0:T(1024)S(1)} %get-tuple-element.854, f32[512]{0:T(512)S(1)} %multiply_reduce_fusion.14, ...), kind=kOutput, calls=%fused_computation.102.clone.1 | convolution fusion | flops 70252544 | bytes 4370436 | tf_op jit(solution)/shard_map/while/body/eval_jaxpr/dot_general | solution.py:108
  138.1 5.6 %all-to-all-start.3 = ((f32[16,2,2048]{2,1,0:T(2,128)}), f32[16,2,2048]{2,1,0:T(2,128)S(1)}, u32[]{:S(2)}, u32[]{:S(2)}) async-start(f32[16,2,2048]{2,1,0:T(2,128)} %broadcast_in_dim.39), calls=%async_computation.3 | async-start | bytes 524288 | tf_op jit(solution)/shard_map/all_to_all | solution.py:18
  143.7 7.7 %all-to-all-done.3 = f32[16,2,2048]{2,1,0:T(2,128)S(1)} async-done(((f32[16,2,2048]{2,1,0:T(2,128)}), f32[16,2,2048]{2,1,0:T(2,128)S(1)}, u32[]{:S(2)}, u32[]{:S(2)}) %all-to-all-start.3) | async-done | bytes 262176 | tf_op jit(solution)/shard_map/all_to_all | solution.py:18
  152.3 18.7 %while.67 = (s32[]{:T(128)}, f32[2048,128]{1,0:T(8,128)S(1)}, f32[2048]{0:T(1024)S(1)}, f32[4,512]{1,0:T(4,128)S(1)}, f32[2048]{0:T(1024)S(1)}, /*index=5*/bf16[...) while((s32[]{:T(128)}, f32[2048,128]{1,0:T(8,128)S(1)}, ...), condition=%wide.region_24.25_spmd.clone, body=%wide.region_21.24_spmd.clone.sunk | while | flops 341359104 | bytes 6668932 | solution.py:197
  174.6 21.9 %all_to_all.31 = f32[16,128,129]{1,2,0:T(8,128)S(1)} all-to-all(f32[16,128,129]{1,2,0:T(8,128)S(1)} %copy.42), channel_id=1, replica_groups=mesh['src'=16,'tgt'=16] {'src'}, dimensions={0} | all-to-all | bytes 2113536 | tf_op jit(solution)/shard_map/all_to_all | solution.py:80
  196.9 18.7 %all_to_all.30 = f32[16,128,128]{2,1,0:T(8,128)S(1)} all-to-all(f32[16,128,128]{2,1,0:T(8,128)S(1)} %broadcast_in_dim.45), channel_id=1, replica_groups=mesh['src'=16,'tgt'=16] {'src'}, dimensions={0} | all-to-all | bytes 2097152 | tf_op jit(solution)/shard_map/all_to_all | solution.py:18
  (227 shorter events, 76.5 us)
Async XLA Ops:
  2.6 33.6 %copy-start = (f32[2048]{0:T(1024)S(1)}, f32[2048]{0:T(1024)}, u32[]{:S(2)}) copy-start(f32[2048]{0:T(1024)} %param.16) | copy-start | bytes 24580
  15.6 19.8 %all-to-all-start = ((f32[16,2,2048]{2,1,0:T(2,128)}), f32[16,2,2048]{2,1,0:T(2,128)S(1)}, u32[]{:S(2)}, u32[]{:S(2)}) async-start(f32[16,2,2048]{2,1,0:T(2,128)} %broadcast_in_dim.36), calls=%async_computation | async-start | bytes 524288 | tf_op jit(solution)/shard_map/all_to_all | solution.py:18
  64.7 15.1 %all-to-all-start.1 = ((f32[16,2,2048]{2,1,0:T(2,128)}), f32[16,2,2048]{2,1,0:T(2,128)S(1)}, u32[]{:S(2)}, u32[]{:S(2)}) async-start(f32[16,2,2048]{2,1,0:T(2,128)} %broadcast_in_dim.37), calls=%async_computation.1 | async-start | bytes 524288 | tf_op jit(solution)/shard_map/all_to_all | solution.py:18
  93.7 14.5 %all-to-all-start.2 = ((f32[16,2,2048]{2,1,0:T(2,128)}), f32[16,2,2048]{2,1,0:T(2,128)S(1)}, u32[]{:S(2)}, u32[]{:S(2)}) async-start(f32[16,2,2048]{2,1,0:T(2,128)} %broadcast_in_dim.38), calls=%async_computation.2 | async-start | bytes 524288 | tf_op jit(solution)/shard_map/all_to_all | solution.py:18
  109.1 0.6 copy-start.1
  138.1 13.3 %all-to-all-start.3 = ((f32[16,2,2048]{2,1,0:T(2,128)}), f32[16,2,2048]{2,1,0:T(2,128)S(1)}, u32[]{:S(2)}, u32[]{:S(2)}) async-start(f32[16,2,2048]{2,1,0:T(2,128)} %broadcast_in_dim.39), calls=%async_computation.3 | async-start | bytes 524288 | tf_op jit(solution)/shard_map/all_to_all | solution.py:18
  171.0 3.6 %copy-start.2 = (f32[2048]{0:T(1024)}, f32[2048]{0:T(1024)S(1)}, u32[]{:S(2)}) copy-start(f32[2048]{0:T(1024)S(1)} %get-tuple-element.914) | copy-start | bytes 24580
where the time goes:
time: 219 us; the launch traced here: 217 us
  matrix products  67.9 us (31%)
  blocking collectives  40.6 us (19%)
  waiting for transfers between devices  37.5 us (17%)
  other arithmetic  31.9 us (15%)
  starting transfers between devices  25 us (11%)
  local copies, waits for them, and re-layouts  11.7 us (5%)
    dot_general x20, matrix products, cost_tile(): lax.dot_general(left, right, (((0,), (0,)), ((), ())), preferred_element_...  60.1 us
    all_to_all x4, waiting for transfers between devices, copy_for_each(): lax.all_to_all(jnp.broadcast_to(x[None], (length, *x.shape)), axis, 0, 0,...  37.5 us
    all_to_all x4, starting transfers between devices, copy_for_each(): lax.all_to_all(jnp.broadcast_to(x[None], (length, *x.shape)), axis, 0, 0,...  25 us
    reduce_sum x8, other arithmetic, column_stats(): jnp.sum(jnp.exp(logits - newpeak[None, :]), axis=0)  22.3 us
    all_to_all x1, blocking collectives, sum_at_owner(): blocks = lax.all_to_all(cut_along(x, dim, length), axis, 0, 0, tiled=True)  21.9 us
    all_to_all x1, blocking collectives, copy_for_each(): lax.all_to_all(jnp.broadcast_to(x[None], (length, *x.shape)), axis, 0, 0,...  18.7 us
    dot_general x4, matrix products, carry_scores(): lax.dot_general(plan.astype(jnp.bfloat16), sblock, (((0,), (0,)), ((), ()...  7.8 us
    reduce_sum x8, other arithmetic, row_stats(): return (peak, jnp.sum(jnp.exp(logits - peak[:, None]), axis=1))  5.69 us
  transfers between devices with their start and end apart: 4, of which 4 were waited for; matrix products, arithmetic and copies ran while one was open for 0% of the time, Pallas kernels for 0%

commit v1 on v0

v1 whole, which is shorter than its diff:
```python
import functools
import math

import jax
import jax.numpy as jnp
from jax import lax
from jax.experimental import pallas as pl
from jax.experimental.pallas import tpu as pltpu
from jax.sharding import PartitionSpec as P

ITERS = 2
EPSILON = 0.05
MARGIN = 1.0
FACTOR = MARGIN / (MARGIN + EPSILON)

UNIT = EPSILON * math.log(2.0)
LOW, HIGH = 2.0**-90, 2.0**100
STATIC, DEPTH = 96, 112
TILE = 256
f32, bf16 = jnp.float32, jnp.bfloat16


def split3(v):
    high = v.astype(bf16).astype(f32)
    rest = v - high
    mid = rest.astype(bf16).astype(f32)
    return high, mid, (rest - mid).astype(bf16).astype(f32)


def rows_of(values, count):
    row = lax.broadcasted_iota(jnp.int32, (count, values[0].shape[-1]), 0)
    out = jnp.zeros(row.shape, f32)
    for k, v in enumerate(values):
        out = jnp.where(row == k, v, out)
    return out.astype(bf16)


def set_source(left, u):
    one = jnp.ones_like(u)
    left[STATIC:, :] = rows_of([*split3(u), one, one, one], DEPTH - STATIC)


def set_target(right, v):
    one = jnp.ones_like(v)
    right[STATIC:, :] = rows_of([one, one, one, *split3(v)], DEPTH - STATIC)


def tile_of(ref, k):
    return ref[:, pl.ds(pl.multiple_of(k * TILE, TILE), TILE)]


def logits(first, second):
    return lax.dot_general(first, second, (((0,), (0,)), ((), ())), preferred_element_type=f32)


def log_sum(first, second):
    count = first.shape[1] // TILE

    def peaks(k, peak):
        return jnp.maximum(peak, jnp.max(logits(tile_of(first, k), second[...]), axis=0, keepdims=True))

    peak = lax.fori_loop(0, count, peaks, jnp.full((1, second.shape[1]), -jnp.inf, f32))

    def totals(k, total):
        part = jnp.exp2(logits(tile_of(first, k), second[...]) - peak)
        return total + jnp.sum(part, axis=0, keepdims=True)

    total = lax.fori_loop(0, count, totals, jnp.zeros_like(peak))
    return peak, total


def merged(parts):
    peak = jnp.max(parts, axis=0)
    return peak + jnp.log2(jnp.sum(jnp.exp2(parts - peak[None]), axis=0))


def in_range(total):
    return jnp.logical_and(jnp.min(total) >= LOW, jnp.max(total) <= HIGH)


def send_copies(out, value):
    out[...] = jnp.broadcast_to(value[None], out.shape)


def weighted(weight, kernel):
    parts = lax.dot_general(
        rows_of(split3(weight), 16), kernel[...], (((1,), (1,)), ((), ())), preferred_element_type=f32
    )
    return jnp.sum(parts[:3], axis=0, keepdims=True)


def first_rows(scale, x_ref, y_ref, s_ref, out, left, right, asq, bsq, shift, kernel, sT, across):
    x = x_ref[...]
    y = y_ref[...].astype(f32)
    xw = x.astype(f32)
    pad = jnp.zeros((32 - x.shape[0], x.shape[1]), f32)
    xp = jnp.concatenate([xw, pad], axis=0).astype(bf16)
    for k, part in enumerate(split3(jnp.concatenate([y * (2.0 * scale), pad], axis=0))):
        left[32 * k : 32 * k + 32, :] = xp
        right[32 * k : 32 * k + 32, :] = part.astype(bf16)
    asq[...] = jnp.sum(xw * xw, axis=0, keepdims=True) * scale
    bsq[...] = jnp.sum(y * y, axis=0, keepdims=True) * scale
    set_source(left, -asq[...])
    set_target(right, -bsq[...])
    across[...] = jnp.transpose(right[...])
    size = x.shape[1]
    chunk = 512
    for n in range(0, size, chunk):
        part = jnp.dot(across[:TILE, :], left[:, n : n + chunk], preferred_element_type=f32)
        shift[:, n : n + chunk] = jnp.max(part, axis=0, keepdims=True)
    set_source(left, -asq[...] - shift[...])
    sums = []
    for n in range(0, size, chunk):
        total = jnp.zeros((8, chunk), f32)
        for k in range(0, size, TILE):
            part = jnp.dot(across[k : k + TILE, :], left[:, n : n + chunk], preferred_element_type=f32)
            part = jnp.exp2(part)
            kernel[k : k + TILE, n : n + chunk] = part.astype(bf16)
            total = total + jnp.sum(part.reshape(TILE // 8, 8, chunk), axis=0)
        sums.append(jnp.sum(total, axis=0, keepdims=True))
    total = jnp.concatenate(sums, axis=1)
    send_copies(out, shift[...] + jnp.log2(total))

    @pl.when(jnp.logical_not(in_range(total)))
    def _():
        set_source(left, -asq[...])
        peak, exact = log_sum(right, left)
        send_copies(out, peak + jnp.log2(exact))

    sT[...] = jnp.transpose(s_ref[...])


def source_weights(log_total, parts, growth, shift):
    rows = merged(parts[...])
    potential = FACTOR * (jnp.log2(growth[...]) - log_total - rows)
    log_weight = potential + shift[...]
    top = jnp.max(log_weight)
    return potential, jnp.exp2(log_weight - top), top


def columns(log_total, parts, growth, shift, kernel, left0, right0, asq, bsq, out, left, right):
    potential, weight, top = source_weights(log_total, parts, growth, shift)
    total = weighted(weight, kernel)
    send_copies(out, top + jnp.log2(total))

    @pl.when(jnp.logical_not(in_range(total)))
    def _():
        left[...] = left0[...]
        right[...] = right0[...]
        set_source(left, potential - asq[...])
        set_target(right, -bsq[...])
        peak, exact = log_sum(left, right)
        send_copies(out, peak + jnp.log2(exact))


def rows(log_total, parts, shift, kernel, left0, right0, asq, bsq, out, left, right):
    potential = FACTOR * (-log_total - merged(parts[...]))
    top = jnp.max(potential)
    weight = jnp.exp2(potential - top)
    parts3 = jnp.dot(rows_of(split3(weight), 16), kernel[...], preferred_element_type=f32)
    total = jnp.sum(parts3[:3], axis=0, keepdims=True)
    send_copies(out, shift[...] + top + jnp.log2(total))

    @pl.when(jnp.logical_not(in_range(total)))
    def _():
        left[...] = left0[...]
        right[...] = right0[...]
        set_source(left, -asq[...])
        set_target(right, potential - bsq[...])
        peak, exact = log_sum(right, left)
        send_copies(out, peak + jnp.log2(exact))


def put_blocks(out, carried, total, peak):
    count, lanes = out.shape[0], out.shape[2]
    progs = carried.shape[0]
    row = lax.broadcasted_iota(jnp.int32, (8, lanes), 0)
    for d in range(count):
        at = slice(d * lanes, (d + 1) * lanes)
        out[d, :progs, :] = carried[:, at]
        extra = jnp.where(row == 0, total[:, at], jnp.where(row == 1, peak[:, at], 0.0))
        out[d, progs:, :] = extra


def carry(log_total, parts, growth, shift, kernel, sT, left0, right0, asq, bsq, fout, out, left, right):
    potential, weight, top = source_weights(log_total, parts, growth, shift)
    fout[...] = potential * UNIT
    total = weighted(weight, kernel)
    scaled = (sT[...].astype(f32) * weight).astype(bf16)
    carried = lax.dot_general(
        scaled, kernel[...], (((1,), (1,)), ((), ())), preferred_element_type=f32
    )
    put_blocks(out, carried, total, jnp.full(total.shape, top, f32))

    @pl.when(jnp.logical_not(in_range(total)))
    def _():
        left[...] = left0[...]
        right[...] = right0[...]
        set_source(left, potential - asq[...])
        set_target(right, -bsq[...])
        peak, exact = log_sum(left, right)

        def step(k, sums):
            plan = jnp.exp2(logits(tile_of(left, k), right[...]) - peak).astype(bf16)
            return sums + jnp.dot(tile_of(sT, k), plan, preferred_element_type=f32)

        sums = lax.fori_loop(0, left.shape[1] // TILE, step, jnp.zeros(carried.shape, f32))
        put_blocks(out, sums, exact, peak)


def finish(log_total, parts, out):
    count, lanes = parts.shape[0], parts.shape[2]
    progs = parts.shape[1] - 8
    peaks = [parts[d, progs + 1 : progs + 2, :] for d in range(count)]
    peak = functools.reduce(jnp.maximum, peaks)
    total = jnp.zeros((1, lanes), f32)
    carried = jnp.zeros((progs, lanes), f32)
    for d in range(count):
        weight = jnp.exp2(peaks[d] - peak)
        total = total + weight * parts[d, progs : progs + 1, :]
        carried = carried + weight * parts[d, :progs, :]
    potential = FACTOR * (-log_total - peak - jnp.log2(total)) * UNIT
    block = jnp.transpose(carried / total)
    extra = jnp.broadcast_to(potential, (8, lanes))
    for d in range(count):
        out[d, :lanes, :] = block
        out[d, lanes:, :] = extra


def call(kernel, outs, scratch=(), flops=10**7, name=None):
    return pl.pallas_call(
        kernel,
        out_shape=outs,
        scratch_shapes=list(scratch),
        compiler_params=pltpu.CompilerParams(vmem_limit_bytes=40 << 20),
        cost_estimate=pl.CostEstimate(flops=flops, bytes_accessed=1 << 20, transcendentals=0),
        name=name,
    )


def exchanged(x, axis):
    return lax.all_to_all(x, axis, 0, 0, tiled=True)


def shards(pcs_source, pcs_target, growth, scores):
    count, size = pcs_source.shape
    progs = scores.shape[1]
    sources, targets = lax.axis_size("src"), lax.axis_size("tgt")
    log_sources = math.log2(size * sources)
    log_targets = math.log2(pcs_target.shape[1] * targets)
    scale = math.log2(math.e) / (EPSILON * count)
    shape = jax.ShapeDtypeStruct
    line = shape((1, size), f32)
    operand = shape((DEPTH, size), bf16)
    operands = [pltpu.VMEM((DEPTH, size), bf16), pltpu.VMEM((DEPTH, size), bf16)]
    to_targets, to_sources = shape((targets, 1, size), f32), shape((sources, 1, size), f32)
    growth = growth.reshape(1, size)

    local, left, right, asq, bsq, shift, kernel, sT = call(
        functools.partial(first_rows, scale),
        (to_targets, operand, operand, line, line, line, shape((size, size), bf16), shape((progs, size), bf16)),
        [pltpu.VMEM((size, DEPTH), bf16)],
        name="first_rows",
    )(pcs_source, pcs_target, scores)
    parts = exchanged(local, "tgt")
    fixed = (left, right, asq, bsq)
    for _ in range(ITERS - 1):
        local = call(functools.partial(columns, log_sources), to_sources, operands, name="columns")(
            parts, growth, shift, kernel, *fixed
        )
        parts = exchanged(local, "src")
        local = call(functools.partial(rows, log_targets), to_targets, operands, name="rows")(
            parts, shift, kernel, *fixed
        )
        parts = exchanged(local, "tgt")
    own = size // sources
    potential, blocks = call(
        functools.partial(carry, log_sources),
        (line, shape((sources, progs + 8, own), f32)),
        operands,
        name="carry",
    )(parts, growth, shift, kernel, sT, *fixed)
    blocks = exchanged(blocks, "src")
    result = call(functools.partial(finish, log_targets), shape((sources, own + 8, progs), f32), name="finish")(blocks)
    result = exchanged(result, "src")
    transported = result[:, :own].reshape(size, progs)
    return potential.reshape(size), result[:, own].reshape(size), transported


def solution(mesh):
    in_specs = (P(None, "src"), P(None, "tgt"), P("src"), P("src", None))
    out_specs = (P("src"), P("tgt"), P("tgt", None))
    return jax.shard_map(shards, mesh=mesh, in_specs=in_specs, out_specs=out_specs, check_vma=False)
```

time: 219 us -> 114 us (0.52)
  the two profiles are of different devices: /device:TPU:8 before, /device:TPU:1 now
where the time goes in v1:
time: 114 us; the launch traced here: 116 us
  blocking collectives  75.4 us (66%)
  Pallas kernels  35.1 us (31%)
  local copies, waits for them, and re-layouts  5.21 us (5%)
    all_to_all x5, blocking collectives, exchanged(): return lax.all_to_all(x, axis, 0, 0, tiled=True)  75.4 us
    pallas_call x1, Pallas kernels, shards(): call(functools.partial(carry, log_sources), (line, shape((sources, progs...  19.7 us
    pallas_call x1, Pallas kernels, shards(): call(functools.partial(columns, log_sources), to_sources, operands, name=...  10.4 us
    unnamed x8, local copies, waits for them, and re-layouts  3.54 us
    pallas_call x1, Pallas kernels, shards(): call(functools.partial(first_rows, scale), (to_targets, operand, operand,...  3.18 us

profile of v1, /device:TPU:1, one launch (start us, length us, event | category | flops | bytes accessed | tf_op | source)
XLA Modules:
  0.0 116.4 jit_solution(5698026032822791909)
XLA Ops:
  0.6 0.0 copy-start
  0.6 1.0 copy-done
  1.7 0.0 copy-start.1
  1.7 0.9 copy-done.1
  2.6 0.0 copy-start.2
  2.6 0.9 copy-done.2
  3.5 3.2 %first_rows.1 = (f32[16,1,2048]{2,1,0:T(1,128)S(1)}, bf16[112,2048]{1,0:T(8,128)(2,1)S(1)}, bf16[112,2048]{1,0:T(8,128)(2,1)S(1)}, f32[1,2048]{1,0:T(1,128)S(1)}...) custom-call(bf16[30,2048]{1,0:T(8,128)(2,1)S(1)} %copy-done.1, ...), custom_call_target="tpu_custom_call" | custom-call | flops 10000000 | bytes 1048576 | tf_op jit(solution)/shard_map/first_rows/pallas_call | solution.py:259
  6.7 18.9 %all_to_all.25.parts = f32[16,1,2048]{2,1,0:T(1,128)S(1)} all-to-all(f32[16,1,2048]{2,1,0:T(1,128)S(1)} %get-tuple-element.13), channel_id=1, replica_groups=mesh['src'=16,'tgt'=16] {'tgt'}, dimensions={0} | all-to-all | bytes 262144 | tf_op jit(solution)/shard_map/all_to_all | solution.py:242
  25.6 0.0 copy-start.3
  25.6 0.7 copy-done.3
  26.3 10.4 %columns.1 = f32[16,1,2048]{2,1,0:T(1,128)S(1)} custom-call(f32[16,1,2048]{2,1,0:T(1,128)S(1)} %all_to_all.25.parts, f32[1,2048]{1,0:T(1,128)S(1)} %bitcast.4, f32[1,2048]{1,0:T(1,128)S(1)} %get-tuple-element.14.shift, bf16[2048,2048]{1,0:T(8,128)(2,1)S(1)} %get-tuple-element.15.kernel, bf16[112,2048]{1,0:T(8,128)(2,1)S(1)} %get-tuple-element.16.left0, ...), custom_call_target="tpu_custom_call" | custom-call | flops 10000000 | bytes 1048576 | tf_op jit(solution)/shard_map/columns/pallas_call | solution.py:268
  36.7 13.4 %all_to_all.26.parts = f32[16,1,2048]{2,1,0:T(1,128)S(1)} all-to-all(f32[16,1,2048]{2,1,0:T(1,128)S(1)} %columns.1), channel_id=1, replica_groups=mesh['src'=16,'tgt'=16] {'src'}, dimensions={0} | all-to-all | bytes 262144 | tf_op jit(solution)/shard_map/all_to_all | solution.py:242
  50.1 1.6 %rows.1 = f32[16,1,2048]{2,1,0:T(1,128)S(1)} custom-call(f32[16,1,2048]{2,1,0:T(1,128)S(1)} %all_to_all.26.parts, f32[1,2048]{1,0:T(1,128)S(1)} %get-tuple-element.14.shift, bf16[2048,2048]{1,0:T(8,128)(2,1)S(1)} %get-tuple-element.15.kernel, bf16[112,2048]{1,0:T(8,128)(2,1)S(1)} %get-tuple-element.16.left0, bf16[112,2048]{1,0:T(8,128)(2,1)S(1)} %get-tuple-element.17.right0, ...), custom_call_target="tpu_custom_call" | custom-call | flops 10000000 | bytes 1048576 | tf_op jit(solution)/shard_map/rows/pallas_call | solution.py:272
  51.7 10.5 %all_to_all.27.parts = f32[16,1,2048]{2,1,0:T(1,128)S(1)} all-to-all(f32[16,1,2048]{2,1,0:T(1,128)S(1)} %rows.1), channel_id=1, replica_groups=mesh['src'=16,'tgt'=16] {'tgt'}, dimensions={0} | all-to-all | bytes 262144 | tf_op jit(solution)/shard_map/all_to_all | solution.py:242
  62.2 19.7 %carry.1 = (f32[1,2048]{1,0:T(1,128)}, f32[16,136,128]{2,1,0:T(8,128)S(1)}) custom-call(f32[16,1,2048]{2,1,0:T(1,128)S(1)} %all_to_all.27.parts, f32[1,2048]{1,0:T(1,128)S(1)} %bitcast.5, f32[1,2048]{1,0:T(1,128)S(1)} %get-tuple-element.14.shift, bf16[2048,2048]{1,0:T(8,128)(2,1)S(1)} %get-tuple-element.15.kernel, ...), custom_call_target="tpu_custom_call" | custom-call | flops 10000000 | bytes 1048576 | tf_op jit(solution)/shard_map/carry/pallas_call | solution.py:277
  81.9 17.4 %all_to_all.28.parts = f32[16,136,128]{2,1,0:T(8,128)S(1)} all-to-all(f32[16,136,128]{2,1,0:T(8,128)S(1)} %get-tuple-element.22), channel_id=1, replica_groups=mesh['src'=16,'tgt'=16] {'src'}, dimensions={0} | all-to-all | bytes 2228224 | tf_op jit(solution)/shard_map/all_to_all | solution.py:242
  99.3 0.2 finish.1
  99.5 15.1 %all_to_all.29 = f32[16,136,128]{2,1,0:T(8,128)S(1)} all-to-all(f32[16,136,128]{2,1,0:T(8,128)S(1)} %finish.1), channel_id=1, replica_groups=mesh['src'=16,'tgt'=16] {'src'}, dimensions={0} | all-to-all | bytes 2228224 | tf_op jit(solution)/shard_map/all_to_all | solution.py:242
  114.7 0.6 slice.8
  115.3 1.1 slice.9
Async XLA Ops:
  0.6 1.0 copy-start
  1.7 0.9 copy-start.1
  2.6 0.9 copy-start.2
  25.6 0.7 copy-start.3
